TPU v7x, 32 devices: a whole 2x2x4 slice. The times are simulated.
32 devices in a mesh: groups: 2 (over y), row: 4 (over x, core), col: 4 (over z).
Axes of the slice: x: 2, y: 2, z: 4, core: 2. Of those that a mesh axis runs over, the one named last changes fastest.
Arguments:
- tiles: float32 [512, 128, 128], P(('groups', 'row', 'col')), parts along dimension 0, may hold values from 0 to 9
- tile_index: int32 [512, 2], P(('groups', 'row', 'col')), parts along dimension 0, may hold values from 0 to 3, as said below
- tile_count: int32 [32], P(('groups', 'row', 'col')), parts along dimension 0, may hold values from 4 to 16, as said below
- sources: int32 [16], P('groups'), parts along dimension 0, may hold values from 0 to 2047
Outputs:
- distance: float32 [16, 2048], P('groups', ('row', 'col')), parts along dimension 0
- path_counts: float32 [16, 2048], P('groups', ('row', 'col')), parts along dimension 0
- centrality: float32 [4096], P(('groups', 'row', 'col')), parts along dimension 0
There are 2 independent parts, one for each index of `groups`. A program takes and returns all parts, laid end to end along the dimension named above; each array names one. Nothing has to cross between parts.
Inputs may be any that keep to these rules, and one draw needn't show every extreme that they name: `tile_index`: entry (r, c) of a slot has r below 4 and c below 4; the 16 slots of one device name distinct pairs. `tile_count`: one entry per device; slots of a device from its count on hold only zeros; some device has all 16 slots live.
All inputs are finite; a program needn't handle non-finite values.
Results may differ from a plain program's by a relative error of at most 0.0003.
Values sent between devices are 32-bit elements; how exact they have to be, the bound alone decides.
A program may use at most 64 MiB of HBM per device.

v0:
```python
import jax
import jax.numpy as jnp
from jax import lax
from jax.sharding import PartitionSpec as P

LEVELS = 3
BACK = 2
far_value = 1000000.0
no_edge = 2000000.0


def combined_all(value, axis, join):
    pieces = jax.tree.map(lambda part: lax.all_gather(part, axis), value)
    head = jax.tree.map(lambda part: part[0], pieces)
    tail = jax.tree.map(lambda part: part[1:], pieces)
    running, _ = lax.scan(lambda running, piece: (join(running, piece), None), head, tail)
    return running


def combine_pair(left_pair, right_pair):
    best_dist = jnp.minimum(left_pair[0], right_pair[0])
    total_count = jnp.where(left_pair[0] == best_dist, left_pair[1], 0.0) + jnp.where(
        right_pair[0] == best_dist, right_pair[1], 0.0
    )
    return (best_dist, total_count)


def pick_rows(band, tile_ids, tile_side):
    source_rows = band.shape[0]
    shaped = band.reshape(source_rows, band.shape[1] // tile_side, tile_side)
    return jnp.take(shaped, tile_ids, axis=1).transpose(1, 0, 2)


def split_blocks(values, tile_side):
    block_size = min(16, tile_side)
    blocks = tile_side // block_size
    return values.reshape(values.shape[0], values.shape[1], blocks, block_size).transpose(
        2, 0, 1, 3
    )


def weight_blocks(weights, tile_side):
    block_size = min(16, tile_side)
    blocks = tile_side // block_size
    return weights.reshape(weights.shape[0], blocks, block_size, tile_side).transpose(1, 0, 2, 3)


def relax_group(near_dist, near_count, weights):
    group, source_rows, tile_side = near_dist.shape

    def advance(carried, pieces):
        dist_part, count_part, weight_part = pieces
        reached = dist_part[:, :, :, None] + weight_part[:, None, :, :]
        best_dist = jnp.min(reached, axis=2)
        total_count = jnp.sum(
            jnp.where(reached == best_dist[:, :, None, :], count_part[:, :, :, None], 0.0), axis=2
        )
        return (combine_pair(carried, (best_dist, total_count)), None)

    initial = (
        jnp.full((group, source_rows, tile_side), far_value, jnp.float32),
        jnp.zeros((group, source_rows, tile_side), jnp.float32),
    )
    result, unused = lax.scan(
        advance,
        initial,
        (
            split_blocks(near_dist, tile_side),
            split_blocks(near_count, tile_side),
            weight_blocks(weights, tile_side),
        ),
    )
    return result


def depend_group(upper_dist, lower_dist, lower_coef, weights):
    group, source_rows, tile_side = upper_dist.shape

    def dependency_rows(pieces):
        upper_part, weight_part = pieces
        reached = upper_part[:, :, :, None] + weight_part[:, None, :, :]
        return jnp.sum(
            jnp.where(reached == lower_dist[:, :, None, :], lower_coef[:, :, None, :], 0.0), axis=3
        )

    row_parts = lax.map(
        dependency_rows, (split_blocks(upper_dist, tile_side), weight_blocks(weights, tile_side))
    )
    return row_parts.transpose(1, 2, 0, 3).reshape(group, source_rows, tile_side)


def per_device(tiles, tile_index, tile_count, sources):
    tile_side = tiles.shape[1]
    slot_total = tiles.shape[0]
    source_rows = sources.shape[0]
    row_count = lax.axis_size("row")
    col_count = lax.axis_size("col")
    my_row = lax.axis_index("row")
    my_col = lax.axis_index("col")
    own_ids = (my_row * col_count + my_col) * tile_side + jnp.arange(tile_side, dtype=jnp.int32)
    own_source = own_ids[None, :] == sources[:, None]
    band_ids = my_row * col_count * tile_side + jnp.arange(col_count * tile_side, dtype=jnp.int32)
    band_source = band_ids[None, :] == sources[:, None]
    live_count = tile_count[0]
    start_dist = jnp.where(own_source, 0.0, far_value).astype(jnp.float32)
    source_ones = jnp.where(own_source, 1.0, 0.0).astype(jnp.float32)
    band_dist = jnp.where(band_source, 0.0, far_value).astype(jnp.float32)
    band_paths = jnp.where(band_source, 1.0, 0.0).astype(jnp.float32)

    def group_parts(start, width):
        slot_ids = start + jnp.arange(width, dtype=jnp.int32)
        live = slot_ids < live_count
        weights = jnp.where((tiles > 0) & live[:, None, None], tiles, no_edge)
        return (weights, tile_index, live)

    def run_groups(process, initial):
        return process(0, slot_total, initial)

    def gather_band(dist_part, path_part):
        return (
            lax.all_gather(dist_part, "col", axis=1, tiled=True),
            lax.all_gather(path_part, "col", axis=1, tiled=True),
        )

    column_tiles = jnp.arange(row_count, dtype=jnp.int32)
    row_tiles = jnp.arange(col_count, dtype=jnp.int32)
    own_dist = start_dist
    own_paths = source_ones
    for level_no in range(LEVELS):
        if level_no > 0:
            band_dist, band_paths = gather_band(own_dist, own_paths)

        def forward_group(start, width, carried, band_dist=band_dist, band_paths=band_paths):
            weights, places, live = group_parts(start, width)
            near_dist = pick_rows(band_dist, places[:, 0], tile_side)
            near_count = pick_rows(band_paths, places[:, 0], tile_side)
            found_dist, found_count = relax_group(near_dist, near_count, weights)
            hits = (places[None, :, 1] == column_tiles[:, None]) & live[None, :]
            masked = jnp.where(hits[:, :, None, None], found_dist[None], far_value)
            best_dist = jnp.min(masked, axis=1)
            total_count = jnp.sum(
                jnp.where(
                    hits[:, :, None, None] & (found_dist[None] == best_dist[:, None]),
                    found_count[None],
                    0.0,
                ),
                axis=1,
            )
            return combine_pair(carried, (best_dist, total_count))

        initial = (
            jnp.full((row_count, source_rows, tile_side), far_value, jnp.float32),
            jnp.zeros((row_count, source_rows, tile_side), jnp.float32),
        )
        folded_dist, folded_count = run_groups(forward_group, initial)
        partial_dist = folded_dist.transpose(1, 0, 2).reshape(source_rows, row_count * tile_side)
        partial_count = folded_count.transpose(1, 0, 2).reshape(source_rows, row_count * tile_side)
        merged = combined_all((partial_dist, partial_count), "row", combine_pair)
        found_dist = lax.dynamic_slice_in_dim(merged[0], my_row * tile_side, tile_side, 1)
        found_count = lax.dynamic_slice_in_dim(merged[1], my_row * tile_side, tile_side, 1)
        own_dist = jnp.minimum(start_dist, found_dist)
        own_paths = source_ones + jnp.where(found_dist == own_dist, found_count, 0.0)
    band_dist, band_paths = gather_band(own_dist, own_paths)
    dependency = jnp.zeros((source_rows, tile_side), jnp.float32)
    for back_no in range(BACK):
        coefficient = jnp.where(
            own_paths > 0.5, (1.0 + dependency) / jnp.maximum(own_paths, 1.0), 0.0
        )
        lower_all, coef_all = (
            lax.all_gather(own_dist, "row", axis=1, tiled=True),
            lax.all_gather(coefficient, "row", axis=1, tiled=True),
        )

        def backward_group(start, width, carried, lower_all=lower_all, coef_all=coef_all):
            weights, places, live = group_parts(start, width)
            upper_dist = pick_rows(band_dist, places[:, 0], tile_side)
            lower_dist = pick_rows(lower_all, places[:, 1], tile_side)
            lower_coef = pick_rows(coef_all, places[:, 1], tile_side)
            dep_terms = depend_group(upper_dist, lower_dist, lower_coef, weights)
            hits = (places[None, :, 0] == row_tiles[:, None]) & live[None, :]
            return carried + jnp.sum(
                jnp.where(hits[:, :, None, None], dep_terms[None], 0.0), axis=1
            )

        folded = run_groups(
            backward_group, jnp.zeros((col_count, source_rows, tile_side), jnp.float32)
        )
        accumulated = folded.transpose(1, 0, 2).reshape(source_rows, col_count * tile_side)
        summed = lax.psum_scatter(accumulated, "col", scatter_dimension=1, tiled=True)
        dependency = own_paths * summed
    centrality = jnp.sum(jnp.where(own_source, 0.0, dependency), axis=0) / source_rows
    shown = jnp.where(own_dist < 0.5 * far_value, own_dist, -1.0)
    return (shown, own_paths, centrality)


def solution(mesh):
    in_specs = (
        P(("groups", "row", "col"), None, None),
        P(("groups", "row", "col"), None),
        P(("groups", "row", "col")),
        P("groups"),
    )
    out_specs = (
        P("groups", ("row", "col")),
        P("groups", ("row", "col")),
        P(("groups", "row", "col")),
    )
    return jax.shard_map(
        per_device, mesh=mesh, in_specs=in_specs, out_specs=out_specs, check_vma=False
    )
```

profile of v0, /device:TPU:0, one launch (start us, length us, event | category | flops | bytes accessed | tf_op | source)
XLA Modules:
  0.0 230.2 jit_solution(145529615375615002)
XLA Ops:
  7.2 0.8 compare_and_fusion
  12.1 9.8 %while.100 = (s32[]{:T(128)}, f32[16,8,128]{2,1,0:T(8,128)S(1)}, f32[16,8,128]{2,1,0:T(8,128)S(1)}, f32[8,16,8,16]{3,0,2,1:T(8,128)S(1)}, f32[8,16,16,128]{3,2,1...) while((s32[]{:T(128)}, f32[16,8,128]{2,1,0:T(8,128)S(1)}, ...), condition=%wide.region_3.5_spmd.clone, body=%wide.region_0.4_spmd.clone.sunk | while | flops 1671171 | bytes 1171559 | solution.py:64
  22.3 6.2 %all_gather.44 = f32[4,8,512]{2,1,0:T(8,128)S(1)} all-gather(f32[1,8,512]{2,1,0:T(8,128)S(1)} %get-tuple-element.541), channel_id=1, replica_groups=mesh['groups'=2,'row'=4,'col'=4] {'row'}, dimensions={0}, use_global_device_ids=true | all-gather | bytes 81920 | tf_op jit(solution)/shard_map/all_gather | solution.py:13
  29.1 5.5 %all_gather.43 = f32[4,8,512]{2,1,0:T(8,128)S(1)} all-gather(f32[1,8,512]{2,1,0:T(8,128)S(1)} %get-tuple-element.542), channel_id=1, replica_groups=mesh['groups'=2,'row'=4,'col'=4] {'row'}, dimensions={0}, use_global_device_ids=true | all-gather | bytes 81920 | tf_op jit(solution)/shard_map/all_gather | solution.py:13
  36.3 13.6 %all_gather.45 = f32[8,512]{1,0:T(8,128)S(1)} all-gather(f32[8,128]{1,0:T(8,128)S(1)} %get-tuple-element.536), channel_id=1, replica_groups=mesh['groups'=2,'row'=4,'col'=4] {'col'}, dimensions={1}, use_global_device_ids=true | all-gather | bytes 20480 | tf_op jit(solution)/shard_map/all_gather | solution.py:121
  50.5 13.2 %all_gather.46 = f32[8,512]{1,0:T(8,128)S(1)} all-gather(f32[8,128]{1,0:T(8,128)S(1)} %get-tuple-element.535), channel_id=1, replica_groups=mesh['groups'=2,'row'=4,'col'=4] {'col'}, dimensions={1}, use_global_device_ids=true | all-gather | bytes 20480 | tf_op jit(solution)/shard_map/all_gather | solution.py:122
  64.7 9.8 %while.101 = (s32[]{:T(128)}, f32[16,8,128]{2,1,0:T(8,128)S(1)}, f32[16,8,128]{2,1,0:T(8,128)S(1)}, f32[8,16,8,16]{3,0,2,1:T(8,128)S(1)}, f32[8,16,16,128]{3,2,1...) while((s32[]{:T(128)}, f32[16,8,128]{2,1,0:T(8,128)S(1)}, ...), condition=%wide.region_11.13_spmd.clone, body=%wide.region_8.12_spmd.clone.sunk | while | flops 1671171 | bytes 1171559 | solution.py:64
  74.8 5.2 %all_gather.48 = f32[4,8,512]{2,1,0:T(8,128)S(1)} all-gather(f32[1,8,512]{2,1,0:T(8,128)S(1)} %get-tuple-element.539), channel_id=1, replica_groups=mesh['groups'=2,'row'=4,'col'=4] {'row'}, dimensions={0}, use_global_device_ids=true | all-gather | bytes 81920 | tf_op jit(solution)/shard_map/all_gather | solution.py:13
  80.7 5.2 %all_gather.47 = f32[4,8,512]{2,1,0:T(8,128)S(1)} all-gather(f32[1,8,512]{2,1,0:T(8,128)S(1)} %get-tuple-element.540), channel_id=1, replica_groups=mesh['groups'=2,'row'=4,'col'=4] {'row'}, dimensions={0}, use_global_device_ids=true | all-gather | bytes 81920 | tf_op jit(solution)/shard_map/all_gather | solution.py:13
  86.0 0.8 slice-done.1
  86.9 13.2 %all_gather.49 = f32[8,512]{1,0:T(8,128)S(1)} all-gather(f32[8,128]{1,0:T(8,128)S(1)} %get-tuple-element.534), channel_id=1, replica_groups=mesh['groups'=2,'row'=4,'col'=4] {'col'}, dimensions={1}, use_global_device_ids=true | all-gather | bytes 20480 | tf_op jit(solution)/shard_map/all_gather | solution.py:121
  100.7 13.2 %all_gather.50 = f32[8,512]{1,0:T(8,128)S(1)} all-gather(f32[8,128]{1,0:T(8,128)S(1)} %get-tuple-element.533), channel_id=1, replica_groups=mesh['groups'=2,'row'=4,'col'=4] {'col'}, dimensions={1}, use_global_device_ids=true | all-gather | bytes 20480 | tf_op jit(solution)/shard_map/all_gather | solution.py:122
  114.9 9.8 %while.102 = (s32[]{:T(128)}, f32[16,8,128]{2,1,0:T(8,128)S(1)}, f32[16,8,128]{2,1,0:T(8,128)S(1)}, f32[8,16,8,16]{3,0,2,1:T(8,128)S(1)}, f32[8,16,16,128]{3,2,1...) while((s32[]{:T(128)}, f32[16,8,128]{2,1,0:T(8,128)S(1)}, ...), condition=%wide.region_19.21_spmd.clone, body=%wide.region_16.20_spmd.clone.sunk | while | flops 1671171 | bytes 1171559 | solution.py:64
  125.0 5.2 %all_gather.52 = f32[4,8,512]{2,1,0:T(8,128)S(1)} all-gather(f32[1,8,512]{2,1,0:T(8,128)S(1)} %get-tuple-element.537), channel_id=1, replica_groups=mesh['groups'=2,'row'=4,'col'=4] {'row'}, dimensions={0}, use_global_device_ids=true | all-gather | bytes 81920 | tf_op jit(solution)/shard_map/all_gather | solution.py:13
  130.9 5.2 %all_gather.51 = f32[4,8,512]{2,1,0:T(8,128)S(1)} all-gather(f32[1,8,512]{2,1,0:T(8,128)S(1)} %get-tuple-element.538), channel_id=1, replica_groups=mesh['groups'=2,'row'=4,'col'=4] {'row'}, dimensions={0}, use_global_device_ids=true | all-gather | bytes 81920 | tf_op jit(solution)/shard_map/all_gather | solution.py:13
  136.1 0.8 slice-done.2
  137.1 13.2 %all_gather.53 = f32[8,512]{1,0:T(8,128)S(1)} all-gather(f32[8,128]{1,0:T(8,128)S(1)} %get-tuple-element.522), channel_id=1, replica_groups=mesh['groups'=2,'row'=4,'col'=4] {'col'}, dimensions={1}, use_global_device_ids=true | all-gather | bytes 20480 | tf_op jit(solution)/shard_map/all_gather | solution.py:121
  150.3 5.2 %all_gather.54 = f32[8,512]{1,0:T(8,128)S(1)} all-gather(f32[8,128]{1,0:T(8,128)S(1)} %get-tuple-element.522), channel_id=1, replica_groups=mesh['groups'=2,'row'=4,'col'=4] {'row'}, dimensions={1}, use_global_device_ids=true | all-gather | bytes 20480 | tf_op jit(solution)/shard_map/all_gather | solution.py:170
  156.1 5.2 %all_gather.55 = f32[8,512]{1,0:T(8,128)S(1)} all-gather(f32[8,128]{1,0:T(8,128)S(1)} %get-tuple-element.520), channel_id=1, replica_groups=mesh['groups'=2,'row'=4,'col'=4] {'row'}, dimensions={1}, use_global_device_ids=true | all-gather | bytes 20480 | tf_op jit(solution)/shard_map/all_gather | solution.py:171
  162.9 6.1 %while.98 = (s32[]{:T(128)}, f32[8,16,8,16]{3,2,1,0:T(8,128)S(1)}, f32[8,16,8,16]{3,2,1,0:T(8,128)S(1)}, f32[8,16,16,128]{3,2,1,0:T(8,128)S(1)}, f32[16,8,128]{2...) while((s32[]{:T(128)}, f32[8,16,8,16]{3,2,1,0:T(8,128)S(1)}, f32[8,16,8,16]{3,2,1,0:T(8,128)S(1)}, ...), condition=%wide.region_26.28_spmd, body=%wide.region_24.27_spmd.sunk | while | flops 1046530 | bytes 688217 | solution.py:86
  170.3 20.4 %reduce-scatter.3.cloned.1.call-done = f32[8,128]{1,0:T(8,128)} async-done(((f32[8,512]{1,0:T(8,128)}), f32[8,128]{1,0:T(8,128)}) %reduce-scatter.3.cloned.1.call-update) | async-done | bytes 4112 | tf_op jit(solution)/shard_map/reduce_scatter | solution.py:189
  191.3 5.2 %all_gather.56 = f32[8,512]{1,0:T(8,128)S(1)} all-gather(f32[8,128]{1,0:T(8,128)S(1)} %divide_select_fusion), channel_id=1, replica_groups=mesh['groups'=2,'row'=4,'col'=4] {'row'}, dimensions={1}, use_global_device_ids=true | all-gather | bytes 20480 | tf_op jit(solution)/shard_map/all_gather | solution.py:171
  197.2 6.1 %while.99 = (s32[]{:T(128)}, f32[8,16,8,16]{3,2,1,0:T(8,128)S(1)}, f32[8,16,8,16]{3,2,1,0:T(8,128)S(1)}, f32[8,16,16,128]{3,2,1,0:T(8,128)S(1)}, f32[16,8,128]{2...) while((s32[]{:T(128)}, f32[8,16,8,16]{3,2,1,0:T(8,128)S(1)}, f32[8,16,8,16]{3,2,1,0:T(8,128)S(1)}, ...), condition=%wide.region_31.33_spmd, body=%wide.region_29.32_spmd.sunk | while | flops 1046530 | bytes 688217 | solution.py:86
  205.2 16.9 %reduce-scatter.5.cloned.1.call-done = f32[8,128]{1,0:T(8,128)} async-done(((f32[8,512]{1,0:T(8,128)}), f32[8,128]{1,0:T(8,128)}) %reduce-scatter.5.cloned.1.call-update) | async-done | bytes 4112 | tf_op jit(solution)/shard_map/reduce_scatter | solution.py:189
  (288 shorter events, 58.9 us)
Async XLA Ops:
  7.2 4.7 %copy-start = (f32[16,128,128]{2,1,0:T(8,128)S(1)}, f32[16,128,128]{2,1,0:T(8,128)}, u32[]{:S(2)}) copy-start(f32[16,128,128]{2,1,0:T(8,128)} %param.22) | copy-start | bytes 3145732
  7.2 183.5 %reduce-scatter.3.cloned.1.call-start = ((), (), s32[]{:S(2)}) async-start(), calls=%async_computation.2 | async-start | bytes 20480 | tf_op jit(solution)/shard_map/reduce_scatter | solution.py:189
  28.5 0.6 copy-start.1
  34.6 0.8 slice-start
  35.5 0.7 copy-start.5
  80.1 0.6 copy-start.2
  85.9 0.8 slice-start.1
  130.3 0.6 copy-start.3
  136.1 0.8 slice-start.2
  137.1 85.0 %copy-start.4 = (f32[8,128]{1,0:T(8,128)}, f32[8,128]{1,0:T(8,128)S(1)}, u32[]{:S(2)}) copy-start(f32[8,128]{1,0:T(8,128)S(1)} %get-tuple-element.521) | copy-start | bytes 12292
  170.3 51.9 %reduce-scatter.5.cloned.1.call-start = ((), (), s32[]{:S(2)}) async-start(), calls=%async_computation.3 | async-start | bytes 20480 | tf_op jit(solution)/shard_map/reduce_scatter | solution.py:189
Sparse Core Ops, SparseCore 0:
  170.4 20.2 reduce-scatter.2
  204.7 17.3 reduce-scatter.4
where the time goes:
time: 231 us; the launch traced here: 230 us
  blocking collectives  115 us (50%)
  other arithmetic  43.7 us (19%)
  waiting for transfers between devices  37.3 us (16%)
  local copies, waits for them, and re-layouts  17.2 us (7%)
  between operations  15.2 us (7%)
    all_gather x3, blocking collectives, gather_band(): lax.all_gather(dist_part, 'col', axis=1, tiled=True)  40 us
    reduce_scatter x2, waiting for transfers between devices, per_device(): lax.psum_scatter(accumulated, 'col', scatter_dimension=1, tiled=True)  37.3 us
    all_gather x6, blocking collectives, combined_all(): pieces = jax.tree.map(lambda part: lax.all_gather(part, axis), value)  32.6 us
    all_gather x2, blocking collectives, gather_band(): lax.all_gather(path_part, 'col', axis=1, tiled=True)  26.4 us
    reduce_sum x24, other arithmetic, advance(): jnp.sum(jnp.where(reached == best_dist[:, :, None, :], count_part[:, :, :...  14.9 us
    reduce_sum x16, other arithmetic, dependency_rows(): jnp.sum(jnp.where(reached == lower_dist[:, :, None, :], lower_coef[:, :,...  10.9 us
    all_gather x2, blocking collectives, per_device(): lax.all_gather(coefficient, 'row', axis=1, tiled=True)  10.4 us
    reduce_min x24, other arithmetic, advance(): best_dist = jnp.min(reached, axis=2)  9.06 us
  transfers between devices with their start and end apart: 2, of which 2 were waited for; matrix products, arithmetic and copies ran while one was open for 0% of the time, Pallas kernels for 0%

commit v1 on v0

--- a/solution.py
+++ b/solution.py
@@ -119,7 +119,7 @@
     def gather_band(dist_part, path_part):
         return (
             lax.all_gather(dist_part, "col", axis=1, tiled=True),
-            lax.all_gather(path_part, "col", axis=1, tiled=True),
+            jnp.concatenate(lax.all_gather(path_part, "col"), axis=1),
         )
 
     column_tiles = jnp.arange(row_count, dtype=jnp.int32)

time: 231 us -> 231 us (level)
  no operation moved by 1% of the time
where the time goes in v1:
time: 231 us; the launch traced here: 230 us
  blocking collectives  115 us (50%)
  other arithmetic  43.7 us (19%)
  waiting for transfers between devices  37.3 us (16%)
  local copies, waits for them, and re-layouts  17.2 us (7%)
  between operations  15.2 us (7%)
    all_gather x3, blocking collectives, gather_band(): lax.all_gather(dist_part, 'col', axis=1, tiled=True)  40 us
    reduce_scatter x2, waiting for transfers between devices, per_device(): lax.psum_scatter(accumulated, 'col', scatter_dimension=1, tiled=True)  37.3 us
    all_gather x6, blocking collectives, combined_all(): pieces = jax.tree.map(lambda part: lax.all_gather(part, axis), value)  32.6 us
    all_gather x2, blocking collectives, gather_band(): lax.all_gather(path_part, 'col')  26.4 us
    reduce_sum x24, other arithmetic, advance(): jnp.sum(jnp.where(reached == best_dist[:, :, None, :], count_part[:, :, :...  14.9 us
    reduce_sum x16, other arithmetic, dependency_rows(): jnp.sum(jnp.where(reached == lower_dist[:, :, None, :], lower_coef[:, :,...  10.9 us
    all_gather x2, blocking collectives, per_device(): lax.all_gather(coefficient, 'row', axis=1, tiled=True)  10.4 us
    reduce_min x24, other arithmetic, advance(): best_dist = jnp.min(reached, axis=2)  9.06 us
  transfers between devices with their start and end apart: 2, of which 2 were waited for; matrix products, arithmetic and copies ran while one was open for 0% of the time, Pallas kernels for 0%

profile of v1, /device:TPU:0, one launch (start us, length us, event | category | flops | bytes accessed | tf_op | source)
XLA Modules:
  0.0 230.2 jit_solution(4931143357158498832)
XLA Ops:
  7.2 0.8 compare_and_fusion
  12.1 9.8 %while.100 = (s32[]{:T(128)}, f32[16,8,128]{2,1,0:T(8,128)S(1)}, f32[16,8,128]{2,1,0:T(8,128)S(1)}, f32[8,16,8,16]{3,0,2,1:T(8,128)S(1)}, f32[8,16,16,128]{3,2,1...) while((s32[]{:T(128)}, f32[16,8,128]{2,1,0:T(8,128)S(1)}, ...), condition=%wide.region_3.5_spmd.clone, body=%wide.region_0.4_spmd.clone.sunk | while | flops 1671171 | bytes 1171559 | solution.py:64
  22.3 6.2 %all_gather.50 = f32[4,8,512]{2,1,0:T(8,128)S(1)} all-gather(f32[1,8,512]{2,1,0:T(8,128)S(1)} %get-tuple-element.541), channel_id=1, replica_groups=mesh['groups'=2,'row'=4,'col'=4] {'row'}, dimensions={0}, use_global_device_ids=true | all-gather | bytes 81920 | tf_op jit(solution)/shard_map/all_gather | solution.py:13
  29.1 5.5 %all_gather.49 = f32[4,8,512]{2,1,0:T(8,128)S(1)} all-gather(f32[1,8,512]{2,1,0:T(8,128)S(1)} %get-tuple-element.542), channel_id=1, replica_groups=mesh['groups'=2,'row'=4,'col'=4] {'row'}, dimensions={0}, use_global_device_ids=true | all-gather | bytes 81920 | tf_op jit(solution)/shard_map/all_gather | solution.py:13
  36.3 13.6 %all_gather.51 = f32[8,512]{1,0:T(8,128)S(1)} all-gather(f32[8,128]{1,0:T(8,128)S(1)} %get-tuple-element.536), channel_id=1, replica_groups=mesh['groups'=2,'row'=4,'col'=4] {'col'}, dimensions={1}, use_global_device_ids=true | all-gather | bytes 20480 | tf_op jit(solution)/shard_map/all_gather | solution.py:121
  50.5 13.2 %all-gather = f32[32,128]{1,0:T(8,128)S(1)} all-gather(f32[8,128]{1,0:T(8,128)S(1)} %get-tuple-element.535), channel_id=2, replica_groups=mesh['groups'=2,'row'=4,'col'=4] {'col'}, dimensions={0}, use_global_device_ids=true | all-gather | bytes 20480 | tf_op jit(solution)/shard_map/all_gather | solution.py:122
  64.7 9.8 %while.101 = (s32[]{:T(128)}, f32[16,8,128]{2,1,0:T(8,128)S(1)}, f32[16,8,128]{2,1,0:T(8,128)S(1)}, f32[8,16,8,16]{3,0,2,1:T(8,128)S(1)}, f32[8,16,16,128]{3,2,1...) while((s32[]{:T(128)}, f32[16,8,128]{2,1,0:T(8,128)S(1)}, ...), condition=%wide.region_11.13_spmd.clone, body=%wide.region_8.12_spmd.clone.sunk | while | flops 1671171 | bytes 1171559 | solution.py:64
  74.8 5.2 %all_gather.55 = f32[4,8,512]{2,1,0:T(8,128)S(1)} all-gather(f32[1,8,512]{2,1,0:T(8,128)S(1)} %get-tuple-element.539), channel_id=1, replica_groups=mesh['groups'=2,'row'=4,'col'=4] {'row'}, dimensions={0}, use_global_device_ids=true | all-gather | bytes 81920 | tf_op jit(solution)/shard_map/all_gather | solution.py:13
  80.7 5.2 %all_gather.54 = f32[4,8,512]{2,1,0:T(8,128)S(1)} all-gather(f32[1,8,512]{2,1,0:T(8,128)S(1)} %get-tuple-element.540), channel_id=1, replica_groups=mesh['groups'=2,'row'=4,'col'=4] {'row'}, dimensions={0}, use_global_device_ids=true | all-gather | bytes 81920 | tf_op jit(solution)/shard_map/all_gather | solution.py:13
  86.0 0.8 slice-done.1
  86.9 13.2 %all_gather.56 = f32[8,512]{1,0:T(8,128)S(1)} all-gather(f32[8,128]{1,0:T(8,128)S(1)} %get-tuple-element.534), channel_id=1, replica_groups=mesh['groups'=2,'row'=4,'col'=4] {'col'}, dimensions={1}, use_global_device_ids=true | all-gather | bytes 20480 | tf_op jit(solution)/shard_map/all_gather | solution.py:121
  100.7 13.2 %all-gather.1 = f32[32,128]{1,0:T(8,128)S(1)} all-gather(f32[8,128]{1,0:T(8,128)S(1)} %get-tuple-element.533), channel_id=3, replica_groups=mesh['groups'=2,'row'=4,'col'=4] {'col'}, dimensions={0}, use_global_device_ids=true | all-gather | bytes 20480 | tf_op jit(solution)/shard_map/all_gather | solution.py:122
  114.9 9.8 %while.102 = (s32[]{:T(128)}, f32[16,8,128]{2,1,0:T(8,128)S(1)}, f32[16,8,128]{2,1,0:T(8,128)S(1)}, f32[8,16,8,16]{3,0,2,1:T(8,128)S(1)}, f32[8,16,16,128]{3,2,1...) while((s32[]{:T(128)}, f32[16,8,128]{2,1,0:T(8,128)S(1)}, ...), condition=%wide.region_19.21_spmd.clone, body=%wide.region_16.20_spmd.clone.sunk | while | flops 1671171 | bytes 1171559 | solution.py:64
  125.0 5.2 %all_gather.60 = f32[4,8,512]{2,1,0:T(8,128)S(1)} all-gather(f32[1,8,512]{2,1,0:T(8,128)S(1)} %get-tuple-element.537), channel_id=1, replica_groups=mesh['groups'=2,'row'=4,'col'=4] {'row'}, dimensions={0}, use_global_device_ids=true | all-gather | bytes 81920 | tf_op jit(solution)/shard_map/all_gather | solution.py:13
  130.9 5.2 %all_gather.59 = f32[4,8,512]{2,1,0:T(8,128)S(1)} all-gather(f32[1,8,512]{2,1,0:T(8,128)S(1)} %get-tuple-element.538), channel_id=1, replica_groups=mesh['groups'=2,'row'=4,'col'=4] {'row'}, dimensions={0}, use_global_device_ids=true | all-gather | bytes 81920 | tf_op jit(solution)/shard_map/all_gather | solution.py:13
  136.1 0.8 slice-done.2
  137.1 13.2 %all_gather.61 = f32[8,512]{1,0:T(8,128)S(1)} all-gather(f32[8,128]{1,0:T(8,128)S(1)} %get-tuple-element.522), channel_id=1, replica_groups=mesh['groups'=2,'row'=4,'col'=4] {'col'}, dimensions={1}, use_global_device_ids=true | all-gather | bytes 20480 | tf_op jit(solution)/shard_map/all_gather | solution.py:121
  150.3 5.2 %all_gather.62 = f32[8,512]{1,0:T(8,128)S(1)} all-gather(f32[8,128]{1,0:T(8,128)S(1)} %get-tuple-element.522), channel_id=1, replica_groups=mesh['groups'=2,'row'=4,'col'=4] {'row'}, dimensions={1}, use_global_device_ids=true | all-gather | bytes 20480 | tf_op jit(solution)/shard_map/all_gather | solution.py:170
  156.1 5.2 %all_gather.63 = f32[8,512]{1,0:T(8,128)S(1)} all-gather(f32[8,128]{1,0:T(8,128)S(1)} %get-tuple-element.520), channel_id=1, replica_groups=mesh['groups'=2,'row'=4,'col'=4] {'row'}, dimensions={1}, use_global_device_ids=true | all-gather | bytes 20480 | tf_op jit(solution)/shard_map/all_gather | solution.py:171
  162.9 6.1 %while.98 = (s32[]{:T(128)}, f32[8,16,8,16]{3,2,1,0:T(8,128)S(1)}, f32[8,16,8,16]{3,2,1,0:T(8,128)S(1)}, f32[8,16,16,128]{3,2,1,0:T(8,128)S(1)}, f32[16,8,128]{2...) while((s32[]{:T(128)}, f32[8,16,8,16]{3,2,1,0:T(8,128)S(1)}, f32[8,16,8,16]{3,2,1,0:T(8,128)S(1)}, ...), condition=%wide.region_26.28_spmd, body=%wide.region_24.27_spmd.sunk | while | flops 1046530 | bytes 688217 | solution.py:86
  170.3 20.4 %reduce-scatter.3.cloned.1.call-done = f32[8,128]{1,0:T(8,128)} async-done(((f32[8,512]{1,0:T(8,128)}), f32[8,128]{1,0:T(8,128)}) %reduce-scatter.3.cloned.1.call-update) | async-done | bytes 4112 | tf_op jit(solution)/shard_map/reduce_scatter | solution.py:189
  191.3 5.2 %all_gather.64 = f32[8,512]{1,0:T(8,128)S(1)} all-gather(f32[8,128]{1,0:T(8,128)S(1)} %divide_select_fusion), channel_id=1, replica_groups=mesh['groups'=2,'row'=4,'col'=4] {'row'}, dimensions={1}, use_global_device_ids=true | all-gather | bytes 20480 | tf_op jit(solution)/shard_map/all_gather | solution.py:171
  197.2 6.1 %while.99 = (s32[]{:T(128)}, f32[8,16,8,16]{3,2,1,0:T(8,128)S(1)}, f32[8,16,8,16]{3,2,1,0:T(8,128)S(1)}, f32[8,16,16,128]{3,2,1,0:T(8,128)S(1)}, f32[16,8,128]{2...) while((s32[]{:T(128)}, f32[8,16,8,16]{3,2,1,0:T(8,128)S(1)}, f32[8,16,8,16]{3,2,1,0:T(8,128)S(1)}, ...), condition=%wide.region_31.33_spmd, body=%wide.region_29.32_spmd.sunk | while | flops 1046530 | bytes 688217 | solution.py:86
  205.2 16.9 %reduce-scatter.5.cloned.1.call-done = f32[8,128]{1,0:T(8,128)} async-done(((f32[8,512]{1,0:T(8,128)}), f32[8,128]{1,0:T(8,128)}) %reduce-scatter.5.cloned.1.call-update) | async-done | bytes 4112 | tf_op jit(solution)/shard_map/reduce_scatter | solution.py:189
  (288 shorter events, 58.9 us)
Async XLA Ops:
  7.2 4.7 %copy-start = (f32[16,128,128]{2,1,0:T(8,128)S(1)}, f32[16,128,128]{2,1,0:T(8,128)}, u32[]{:S(2)}) copy-start(f32[16,128,128]{2,1,0:T(8,128)} %param.22) | copy-start | bytes 3145732
  7.2 183.5 %reduce-scatter.3.cloned.1.call-start = ((), (), s32[]{:S(2)}) async-start(), calls=%async_computation.2 | async-start | bytes 20480 | tf_op jit(solution)/shard_map/reduce_scatter | solution.py:189
  28.5 0.6 copy-start.1
  34.6 0.8 slice-start
  35.5 0.7 copy-start.5
  80.1 0.6 copy-start.2
  85.9 0.8 slice-start.1
  130.3 0.6 copy-start.3
  136.1 0.8 slice-start.2
  137.1 85.0 %copy-start.4 = (f32[8,128]{1,0:T(8,128)}, f32[8,128]{1,0:T(8,128)S(1)}, u32[]{:S(2)}) copy-start(f32[8,128]{1,0:T(8,128)S(1)} %get-tuple-element.521) | copy-start | bytes 12292
  170.3 51.9 %reduce-scatter.5.cloned.1.call-start = ((), (), s32[]{:S(2)}) async-start(), calls=%async_computation.3 | async-start | bytes 20480 | tf_op jit(solution)/shard_map/reduce_scatter | solution.py:189
Sparse Core Ops, SparseCore 0:
  170.4 20.2 reduce-scatter.2
  204.7 17.3 reduce-scatter.4
